TPU v7x, 32 devices: a whole 2x2x4 slice. The times are simulated.
32 devices in a mesh: section: 4 (over x, core), expert: 8 (over z, y).
Axes of the slice: x: 2, y: 2, z: 4, core: 2. Of those that a mesh axis runs over, the one named last changes fastest.
Arguments:
- grad_rows: bfloat16 [4, 2, 1024, 1024], P('section', None, 'expert'), may hold values from -1 to 1
- owner_ids: int32 [4, 2, 1024, 1], P('section', None, 'expert'), may hold values from 0 to 7; in each aligned block of 128 rows (0 to 127, 128 to 255, ..., all dimensions but the last counted through in order) at most 32 rows name the same one
- saved_hidden: bfloat16 [4, 2, 8, 256, 384], P('section', None, 'expert'), may hold values from -6 to 6
- momentum: bfloat16 [4, 8, 384, 1024], P('section', 'expert'), may hold values from -32 to 32
Outputs:
- new_momentum: bfloat16 [4, 8, 384, 1024], P('section', 'expert')
- update_step: bfloat16 [4, 8, 384, 1024], P('section', 'expert')
Inputs may be any that keep to these rules, and one draw needn't show every extreme that they name: `owner_ids`: within each aligned block of 128 rows of one section and direction, no owner is named by more than 32 rows, a bound that some block reaches.
All inputs are finite; a program needn't handle non-finite values.
Results may differ from a plain program's by a relative error of at most 0.0065.
Values may be sent and summed in bfloat16 or wider, within the bound.
No kernel may reach another device: no remote copies, remote signals or barrier semaphores. Data moves between devices by JAX's collectives and lax.ppermute only.
A program may use at most 64 MiB of HBM per device.

v0:
```python
import functools
import math

import jax
import jax.numpy as jnp
from jax import lax
from jax.experimental import pallas as pl
from jax.experimental.pallas import tpu as pltpu
from jax.sharding import PartitionSpec as P

ITERS = 2
TILE_ROWS = 16
PIECES = 1

momentum_decay = 0.95
coef_first = 3.4445
coef_second = -4.775
coef_third = 2.0315
norm_epsilon = 1e-06

VMEM = pl.BlockSpec(memory_space=pltpu.VMEM)
ANY = pl.BlockSpec(memory_space=pl.ANY)


def whole_call(body, out_shape, operands, scratch=(), in_spec=VMEM, out_spec=VMEM):
    return pl.pallas_call(
        body,
        out_shape=out_shape,
        in_specs=[in_spec] * len(operands),
        out_specs=out_spec if isinstance(out_spec, tuple) else (out_spec,) * len(out_shape) if isinstance(out_shape, tuple) else out_spec,
        scratch_shapes=list(scratch),
    )(*operands)


def in_vmem(array):
    return pltpu.with_memory_space_constraint(array, pltpu.VMEM)


def own_half(sections):
    return (lax.axis_index("section") >= sections // 2).astype(jnp.int32)


def placement(owners, slots, capacity):
    count = owners.shape[1]
    peers = slots // capacity
    earlier = (
        lax.broadcasted_iota(jnp.int32, (count, count), 0)
        < lax.broadcasted_iota(jnp.int32, (count, count), 1)
    ).astype(jnp.bfloat16)
    onehot = lax.broadcasted_iota(jnp.int32, (peers, count), 0) == owners
    before = jnp.dot(onehot.astype(jnp.bfloat16), earlier, preferred_element_type=jnp.float32)
    within = jnp.sum(jnp.where(onehot, before, 0.0), axis=0, keepdims=True)
    target = owners * capacity + within.astype(jnp.int32)
    return (lax.broadcasted_iota(jnp.int32, (slots, count), 0) == target).astype(jnp.bfloat16)


def place(matrix, rows):
    return jnp.dot(matrix, rows, preferred_element_type=jnp.float32).astype(jnp.bfloat16)


def pack_kernel(peers, capacity, sections, ids_ref, rows_ref, out_ref):
    half = own_half(sections)
    for direction in range(2):
        packed = place(placement(ids_ref[direction], peers * capacity, capacity), rows_ref[direction])
        out_ref[half if direction == 0 else 1 - half] = packed


def pack_split_kernel(peers, capacity, sections, ids_hbm, rows_hbm, hidden_hbm, joint_hbm, *refs):
    near_peers = peers // 2
    part = near_peers * capacity
    pairs = near_peers // 2
    *single_refs, near_out, far_out, ids, rows, hidden, joint, sems = refs
    count = rows.shape[1]
    step = count // PIECES
    ids_copy = pltpu.make_async_copy(ids_hbm, ids, sems.at[0, 0])
    ids_copy.start()
    row_copies = []
    for direction in range(2):
        for piece in range(PIECES):
            span = pl.ds(piece * step, step)
            copy = pltpu.make_async_copy(
                rows_hbm.at[direction, span], rows.at[direction, span], sems.at[1 + direction, piece]
            )
            copy.start()
            row_copies.append(copy)
    hidden_copies = [
        pltpu.make_async_copy(hidden_hbm.at[direction], hidden.at[direction], sems.at[4, direction])
        for direction in range(2)
    ]
    for copy in hidden_copies:
        copy.start()
    half = own_half(sections)
    me = lax.axis_index("expert")
    ids_copy.wait()
    matrices = []
    for direction in range(2):
        owners = ids[direction]
        distance = owners ^ me
        joint_xor = direction * near_peers
        inside = jnp.where((distance & near_peers) == joint_xor, owners & (near_peers - 1),
                           near_peers + (distance & (near_peers - 1)))
        matrices.append(placement(inside, peers * capacity, capacity))
    out_copies = []
    for direction in range(2):
        for copy in row_copies[direction * PIECES : (direction + 1) * PIECES]:
            copy.wait()
        joint[direction] = place(matrices[direction][:part], rows[direction])
        copy = pltpu.make_async_copy(
            joint.at[direction],
            joint_hbm.at[half if direction == 0 else 1 - half],
            sems.at[3, direction],
        )
        copy.start()
        out_copies.append(copy)
    for direction in range(2):
        packed = place(matrices[direction][part:], rows[direction])
        offset = 0
        for ref in single_refs[:pairs] if direction == 0 else single_refs[pairs:]:
            ref[...] = packed[offset : offset + ref.shape[0]]
            offset += ref.shape[0]
    own_part = me & near_peers
    for direction, out_ref in ((0, near_out), (1, far_out)):
        hidden_copies[direction].wait()
        first = own_part if direction == 0 else near_peers - own_part
        blocks = [hidden[direction, pl.ds(pl.multiple_of(first * capacity, part), part), :]]
        for index in range(near_peers):
            source = me ^ (index + near_peers if direction == 0 else index)
            start = pl.multiple_of(source * capacity, capacity)
            blocks.append(hidden[direction, pl.ds(start, capacity), :])
        out_ref[...] = jnp.concatenate(blocks, axis=0).T
    for copy in out_copies:
        copy.wait()


def contract(hidden_block, grad_block):
    return lax.dot_general(
        hidden_block, grad_block, (((0,), (0,)), ((), ())), preferred_element_type=jnp.float32
    ).astype(jnp.bfloat16).astype(jnp.float32)


def update(read_rows, near_ref, far_ref, momentum_ref, new_ref, step_ref, current):
    height, width = momentum_ref.shape
    chunk = min(256, width)
    columns = [pl.ds(start, chunk) for start in range(0, width, chunk)]
    squares = jnp.zeros((8, chunk), jnp.float32)
    for cols in columns:
        accum = momentum_decay * momentum_ref[:, cols].astype(jnp.float32)
        accum += contract(near_ref[...], read_rows(0, cols))
        accum += contract(far_ref[...], read_rows(1, cols))
        current[:, cols] = accum
        squares += jnp.sum((accum * accum).reshape(height // 8, 8, chunk), axis=0)
        new_ref[:, cols] = accum.astype(jnp.bfloat16)
    inverse = 1.0 / (jnp.sqrt(jnp.sum(squares)) + norm_epsilon)
    for cols in columns:
        step_ref[:, cols] = (current[:, cols] * inverse).astype(jnp.bfloat16)
    for iteration in range(ITERS):
        whole = step_ref[...]
        gram = lax.dot_general(
            whole, whole, (((1,), (1,)), ((), ())), preferred_element_type=jnp.float32
        ).astype(jnp.bfloat16)
        square = jnp.dot(gram, gram, preferred_element_type=jnp.float32)
        factor = (coef_second * gram.astype(jnp.float32) + coef_third * square).astype(
            jnp.bfloat16
        )
        for cols in columns:
            block = step_ref[:, cols]
            applied = jnp.dot(factor, block, preferred_element_type=jnp.float32)
            combined = coef_first * block.astype(jnp.float32) + applied
            if iteration == ITERS - 1:
                combined = combined * math.sqrt(width)
            step_ref[:, cols] = combined.astype(jnp.bfloat16)


def finish_kernel(sections, rows_ref, near_ref, far_ref, momentum_ref, new_ref, step_ref, current):
    half = own_half(sections)

    def read_rows(direction, cols):
        return rows_ref[half if direction == 0 else 1 - half, :, cols]

    update(read_rows, near_ref, far_ref, momentum_ref, new_ref, step_ref, current)


def finish_split_kernel(peers, sections, joint_ref, *refs):
    near_peers = peers // 2
    pairs = near_peers // 2
    pair_refs, relay_refs, single_refs = refs[:pairs], refs[pairs : 2 * pairs], refs[2 * pairs : 4 * pairs]
    near_ref, far_ref, momentum_ref, new_hbm, step_hbm, new_ref, step_ref, sems = refs[4 * pairs :]
    capacity = relay_refs[0].shape[0]
    half = own_half(sections)
    height, width = momentum_ref.shape
    chunk = min(256, width)
    columns = [pl.ds(start, chunk) for start in range(0, width, chunk)]

    def copies(ref, hbm, row):
        return [
            pltpu.make_async_copy(ref.at[:, cols], hbm.at[:, cols], sems.at[row, index])
            for index, cols in enumerate(columns)
        ]

    new_copies, step_copies = copies(new_ref, new_hbm, 0), copies(step_ref, step_hbm, 1)
    hidden = jnp.concatenate([near_ref[...], far_ref[...]], axis=1)
    for cols, copy in zip(columns, new_copies):
        rows = jnp.concatenate(
            [joint_ref[half, :, cols]]
            + [
                block
                for pair, relay in zip(pair_refs, relay_refs)
                for block in (pair[:capacity, cols], relay[:, cols])
            ]
            + [joint_ref[1 - half, :, cols]]
            + [ref[:, cols] for ref in single_refs],
            axis=0,
        )
        accum = jnp.dot(hidden, rows, preferred_element_type=jnp.float32)
        accum += momentum_decay * momentum_ref[:, cols].astype(jnp.float32)
        new_ref[:, cols] = accum.astype(jnp.bfloat16)
        copy.start()
    squares = jnp.zeros((8, chunk), jnp.float32)
    for cols in columns:
        block = new_ref[:, cols].astype(jnp.float32)
        squares += jnp.sum((block * block).reshape(height // 8, 8, chunk), axis=0)
    inverse = 1.0 / (jnp.sqrt(jnp.sum(squares)) + norm_epsilon)
    for iteration in range(ITERS):
        source_ref = new_ref if iteration == 0 else step_ref
        whole = source_ref[...]
        gram = lax.dot_general(whole, whole, (((1,), (1,)), ((), ())), preferred_element_type=jnp.float32)
        scale = coef_first
        if iteration == 0:
            gram = gram * (inverse * inverse)
            scale = scale * inverse
        if iteration == ITERS - 1:
            scale = scale * math.sqrt(width)
        gram = gram.astype(jnp.bfloat16)
        square = jnp.dot(gram, gram, preferred_element_type=jnp.float32)
        factor = (
            (coef_second / coef_first) * gram.astype(jnp.float32) + (coef_third / coef_first) * square
        ).astype(jnp.bfloat16)
        for cols, copy in zip(columns, step_copies):
            block = source_ref[:, cols]
            applied = jnp.dot(factor, block, preferred_element_type=jnp.float32)
            step_ref[:, cols] = (scale * (block.astype(jnp.float32) + applied)).astype(jnp.bfloat16)
            if iteration == ITERS - 1:
                copy.start()
    for copy in new_copies + step_copies:
        copy.wait()


def joint_groups(sections, peers, split):
    mirror = lambda section: sections - 1 - section
    if not split:
        return [
            [section * peers + expert for section in (first, mirror(first)) for expert in range(peers)]
            for first in range(sections // 2)
        ]
    count = peers // 2
    return [
        [first * peers + part * count + index for index in range(count)]
        + [mirror(first) * peers + (1 - part) * count + index for index in range(count)]
        for first in range(sections // 2)
        for part in range(2)
    ]


def direct(block, sections, peers, distance, crossing):
    pairs = [
        (
            section * peers + expert,
            (sections - 1 - section if crossing else section) * peers + (expert ^ distance),
        )
        for section in range(sections)
        for expert in range(peers)
    ]
    return lax.ppermute(block, ("section", "expert"), pairs)


def exchange(blocks, groups):
    return lax.all_to_all(
        blocks, ("section", "expert"), split_axis=0, concat_axis=0, axis_index_groups=groups, tiled=True
    )


def splits(peers, capacity):
    return peers > 2 and peers & (peers - 1) == 0 and capacity % TILE_ROWS == 0


def per_device(grad_rows, owner_ids, saved_hidden, momentum):
    sections = lax.axis_size("section")
    peers = lax.axis_size("expert")
    slots = saved_hidden.shape[3]
    capacity = slots // peers
    count, width = grad_rows.shape[2:]
    ids = owner_ids[0].reshape(2, 1, count)
    shaped = lambda *shape: jax.ShapeDtypeStruct(shape, jnp.bfloat16)
    landing = lambda *shape: pltpu.VMEM(shape, jnp.bfloat16)
    last = (saved_hidden[0, 0, 0], momentum[0, 0])
    outs = (shaped(*momentum.shape[2:]),) * 2
    current = pltpu.VMEM(momentum.shape[2:], jnp.float32)
    split = splits(peers, capacity)
    groups = joint_groups(sections, peers, split)

    def hidden_over(hidden):
        return lax.ppermute(hidden, "section", [(i, sections - 1 - i) for i in range(sections)])

    if not split:
        packed = whole_call(
            functools.partial(pack_kernel, peers, capacity, sections),
            shaped(2, slots, width), (ids, grad_rows[0]),
        )
        arrived = exchange(packed.reshape(2 * peers, capacity, width), groups).reshape(2, slots, width)
        operands = (arrived, last[0], hidden_over(saved_hidden[0, 1, 0]), last[1])
        body = functools.partial(finish_kernel, sections)
        scratch = (current,)
    else:
        near_peers = peers // 2
        height = saved_hidden.shape[4]
        joint, *singles, near_hidden, turned = whole_call(
            functools.partial(pack_split_kernel, peers, capacity, sections),
            (shaped(2, near_peers * capacity, width),) + (landing(2 * capacity, width),) * (near_peers // 2)
            + (landing(capacity, width),) * near_peers
            + (landing(height, slots),) * 2,
            (ids, grad_rows[0], saved_hidden.reshape(2, slots, height)),
            (
                pltpu.VMEM(ids.shape, jnp.int32),
                pltpu.VMEM(grad_rows.shape[1:], jnp.bfloat16),
                pltpu.VMEM((2, slots, height), jnp.bfloat16),
                pltpu.VMEM((2, near_peers * capacity, width), jnp.bfloat16),
                pltpu.SemaphoreType.DMA((5, 2)),
            ),
            in_spec=ANY,
            out_spec=(ANY,) + (VMEM,) * (near_peers // 2 + near_peers + 2),
        )
        pairs = near_peers // 2
        landed, relayed, mirrored = [], [], []
        for index, block in enumerate(singles[:pairs]):
            landed.append(direct(block, sections, peers, near_peers + 2 * index, False))
        for index, block in enumerate(singles[pairs:]):
            mirrored.append(direct(block, sections, peers, index, True))
        for block in landed:
            relayed.append(direct(block[capacity:], sections, peers, 1, False))
        far_hidden = hidden_over(turned)
        arrived = exchange(joint.reshape(peers, capacity, width), groups)
        operands = (arrived.reshape(joint.shape), *landed, *relayed, *mirrored, near_hidden, far_hidden, last[1])
        body = functools.partial(finish_split_kernel, peers, sections)
        scratch = (
            pltpu.VMEM(momentum.shape[2:], jnp.bfloat16),
            pltpu.VMEM(momentum.shape[2:], jnp.bfloat16),
            pltpu.SemaphoreType.DMA((2, pl.cdiv(width, 256))),
        )
    new_momentum, update_step = whole_call(
        body, outs, tuple(map(in_vmem, operands)), scratch,
        out_spec=ANY if split else VMEM,
    )
    return (new_momentum[None, None], update_step[None, None])


def solution(mesh):
    placed = (
        P("section", None, "expert", None),
        P("section", None, "expert", None),
        P("section", None, "expert", None, None),
        P("section", "expert", None, None),
    )

    return jax.shard_map(
        per_device,
        mesh=mesh,
        in_specs=placed,
        out_specs=(P("section", "expert", None, None), P("section", "expert", None, None)),
        check_vma=False,
    )
```

profile of v0, /device:TPU:0, one launch (start us, length us, event | category | flops | bytes accessed | tf_op | source)
XLA Modules:
  0.0 48.5 jit_solution(8126518344103230688)
XLA Ops:
  0.6 2.2 %shard_map.59 = (bf16[2,128,1024]{2,1,0:T(8,128)(2,1)}, bf16[64,1024]{1,0:T(8,128)(2,1)S(1)}, bf16[64,1024]{1,0:T(8,128)(2,1)S(1)}, bf16[32,1024]{1,0:T(8,128)(2...) custom-call(s32[2,1,128]{2,1,0:T(1,128)} %bitcast.13, ...), custom_call_target="tpu_custom_call" | custom-call | tf_op jit(solution)/shard_map/pallas_call | solution.py:26
  2.8 0.0 copy-start
  2.8 7.8 %all-to-all-start = ((bf16[8,32,1024]{2,1,0:T(8,128)(2,1)}), bf16[8,32,1024]{2,1,0:T(8,128)(2,1)S(1)}, u32[]{:S(2)}, u32[]{:S(2)}) async-start(bf16[8,32,1024]{2,1,0:T(8,128)(2,1)} %bitcast.11), calls=%async_computation | async-start | bytes 1048576 | tf_op jit(solution)/shard_map/all_to_all | solution.py:277
  10.7 0.2 collective-permute-start
  10.9 4.2 %collective-permute-start.1 = (bf16[64,1024]{1,0:T(8,128)(2,1)S(1)}, bf16[64,1024]{1,0:T(8,128)(2,1)S(1)}, u32[]{:S(2)}, u32[]{:S(2)}) collective-permute-start(bf16[64,1024]{1,0:T(8,128)(2,1)S(1)} %get-tuple-element.15), channel_id=1, source_target_pairs={{0,6},{1,7},{2,4},{3,5},{4,2},{5,3},{6,0},{7,1},{8,14},{9,15},{10,... | collective-permute-start | bytes 393224 | tf_op jit(solution)/shard_map/ppermute | solution.py:273
  15.0 0.3 collective-permute-start.8
  15.4 1.4 %collective-permute-start.4 = (bf16[32,1024]{1,0:T(8,128)(2,1)S(1)}, bf16[32,1024]{1,0:T(8,128)(2,1)S(1)}, u32[]{:S(2)}, u32[]{:S(2)}) collective-permute-start(bf16[32,1024]{1,0:T(8,128)(2,1)S(1)} %get-tuple-element.16), channel_id=1, source_target_pairs={{0,24},{1,25},{2,26},{3,27},{4,28},{5,29},{6,30},{7,31},{8,16},{9,... | collective-permute-start | bytes 196616 | tf_op jit(solution)/shard_map/ppermute | solution.py:273
  16.8 1.2 %collective-permute-start.5 = (bf16[32,1024]{1,0:T(8,128)(2,1)S(1)}, bf16[32,1024]{1,0:T(8,128)(2,1)S(1)}, u32[]{:S(2)}, u32[]{:S(2)}) collective-permute-start(bf16[32,1024]{1,0:T(8,128)(2,1)S(1)} %get-tuple-element.17), channel_id=1, source_target_pairs={{0,25},{1,24},{2,27},{3,26},{4,29},{5,28},{6,31},{7,30},{8,17},{9,... | collective-permute-start | bytes 196616 | tf_op jit(solution)/shard_map/ppermute | solution.py:273
  18.0 14.2 %collective-permute-done.refs_0_ = bf16[64,1024]{1,0:T(8,128)(2,1)S(1)} collective-permute-done((bf16[64,1024]{1,0:T(8,128)(2,1)S(1)}, bf16[64,1024]{1,0:T(8,128)(2,1)S(1)}, u32[]{:S(2)}, u32[]{:S(2)}) %collective-permute-start) | collective-permute-done | bytes 131104 | tf_op jit(solution)/shard_map/ppermute | solution.py:273
  32.3 0.1 collective-permute-start.6
  32.3 0.0 collective-permute-done.1.refs_1_
  32.3 6.1 %collective-permute-start.7 = (bf16[32,1024]{1,0:T(8,128)(2,1)S(1)}, bf16[32,1024]{1,0:T(8,128)(2,1)S(1)}, u32[]{:S(2)}, u32[]{:S(2)}) collective-permute-start(bf16[32,1024]{1,0:T(8,128)(2,1)S(1)} %get-tuple-element.19), channel_id=1, source_target_pairs={{0,27},{1,26},{2,25},{3,24},{4,31},{5,30},{6,29},{7,28},{8,19},{9,... | collective-permute-start | bytes 196616 | tf_op jit(solution)/shard_map/ppermute | solution.py:273
  38.5 0.0 collective-permute-done.4.refs_4_
  38.5 0.6 %collective-permute-start.2 = (bf16[32,1024]{1,0:T(8,128)(2,1)S(1)}, bf16[32,1024]{1,0:T(8,128)(2,1)S(1)}, u32[]{:S(2)}, u32[]{:S(2)}) collective-permute-start(bf16[32,1024]{1,0:T(8,128)(2,1)S(1)} %slice.8), channel_id=1, source_target_pairs={{0,1},{1,0},{2,3},{3,2},{4,5},{5,4},{6,7},{7,6},{8,9},{9,8},{10,11... | collective-permute-start | bytes 196616 | tf_op jit(solution)/shard_map/ppermute | solution.py:273
  39.1 0.0 collective-permute-done.5.refs_5_
  39.1 1.5 %collective-permute-start.3 = (bf16[32,1024]{1,0:T(8,128)(2,1)S(1)}, bf16[32,1024]{1,0:T(8,128)(2,1)S(1)}, u32[]{:S(2)}, u32[]{:S(2)}) collective-permute-start(bf16[32,1024]{1,0:T(8,128)(2,1)S(1)} %slice.9), channel_id=1, source_target_pairs={{0,1},{1,0},{2,3},{3,2},{4,5},{5,4},{6,7},{7,6},{8,9},{9,8},{10,11... | collective-permute-start | bytes 196616 | tf_op jit(solution)/shard_map/ppermute | solution.py:273
  40.6 0.0 collective-permute-done.6.refs_6_
  40.6 0.0 collective-permute-done.7.refs_7_
  40.6 2.6 %collective-permute-done.2.refs_2_ = bf16[32,1024]{1,0:T(8,128)(2,1)S(1)} collective-permute-done((bf16[32,1024]{1,0:T(8,128)(2,1)S(1)}, bf16[32,1024]{1,0:T(8,128)(2,1)S(1)}, u32[]{:S(2)}, u32[]{:S(2)}) %collective-permute-start.2) | collective-permute-done | bytes 65568 | tf_op jit(solution)/shard_map/ppermute | solution.py:273
  43.2 1.4 %collective-permute-done.3.refs_3_ = bf16[32,1024]{1,0:T(8,128)(2,1)S(1)} collective-permute-done((bf16[32,1024]{1,0:T(8,128)(2,1)S(1)}, bf16[32,1024]{1,0:T(8,128)(2,1)S(1)}, u32[]{:S(2)}, u32[]{:S(2)}) %collective-permute-start.3) | collective-permute-done | bytes 65568 | tf_op jit(solution)/shard_map/ppermute | solution.py:273
  44.6 0.0 collective-permute-done.8.refs_9_
  44.6 0.0 all-to-all-done
  44.6 0.0 copy-done
  44.6 3.9 %shard_map.60 = (bf16[384,1024]{1,0:T(8,128)(2,1)}, bf16[384,1024]{1,0:T(8,128)(2,1)}) custom-call(bf16[2,128,1024]{2,1,0:T(8,128)(2,1)S(1)} %bitcast.8, bf16[64,1024]{1,0:T(8,128)(2,1)S(1)} %collective-permute-done.refs_0_, bf16[64,1024]{1,0:T(8,128)(2,1)S(1)} %collective-permute-done.1.refs_1_, bf16[32,1024]{1,0:T(8,128)(2,1)S(1)} %collective-permute-done.2.refs_2_, ...), custom_call_target="tpu_custom_call" | custom-call | tf_op jit(solution)/shard_map/pallas_call | solution.py:26
  (2 shorter events, 0.0 us)
Async XLA Ops:
  2.8 41.8 %copy-start = (bf16[1,1,384,1024]{3,2,1,0:T(8,128)(2,1)S(1)}, bf16[1,1,384,1024]{3,2,1,0:T(8,128)(2,1)}, u32[]{:S(2)}) copy-start(bf16[1,1,384,1024]{3,2,1,0:T(8,128)(2,1)} %param.7) | copy-start | bytes 2359300
  2.8 41.8 %all-to-all-start = ((bf16[8,32,1024]{2,1,0:T(8,128)(2,1)}), bf16[8,32,1024]{2,1,0:T(8,128)(2,1)S(1)}, u32[]{:S(2)}, u32[]{:S(2)}) async-start(bf16[8,32,1024]{2,1,0:T(8,128)(2,1)} %bitcast.11), calls=%async_computation | async-start | bytes 1048576 | tf_op jit(solution)/shard_map/all_to_all | solution.py:277
  10.7 21.6 %collective-permute-start = (bf16[64,1024]{1,0:T(8,128)(2,1)S(1)}, bf16[64,1024]{1,0:T(8,128)(2,1)S(1)}, u32[]{:S(2)}, u32[]{:S(2)}) collective-permute-start(bf16[64,1024]{1,0:T(8,128)(2,1)S(1)} %get-tuple-element.14), channel_id=1, source_target_pairs={{0,4},{1,5},{2,6},{3,7},{4,0},{5,1},{6,2},{7,3},{8,12},{9,13},{10,... | collective-permute-start | bytes 393224 | tf_op jit(solution)/shard_map/ppermute | solution.py:273
  10.9 21.5 %collective-permute-start.1 = (bf16[64,1024]{1,0:T(8,128)(2,1)S(1)}, bf16[64,1024]{1,0:T(8,128)(2,1)S(1)}, u32[]{:S(2)}, u32[]{:S(2)}) collective-permute-start(bf16[64,1024]{1,0:T(8,128)(2,1)S(1)} %get-tuple-element.15), channel_id=1, source_target_pairs={{0,6},{1,7},{2,4},{3,5},{4,2},{5,3},{6,0},{7,1},{8,14},{9,15},{10,... | collective-permute-start | bytes 393224 | tf_op jit(solution)/shard_map/ppermute | solution.py:273
  15.0 29.6 %collective-permute-start.8 = (bf16[384,256]{1,0:T(8,128)(2,1)S(1)}, bf16[384,256]{1,0:T(8,128)(2,1)S(1)}, u32[]{:S(2)}, u32[]{:S(2)}) collective-permute-start(bf16[384,256]{1,0:T(8,128)(2,1)S(1)} %get-tuple-element.21), channel_id=1, source_target_pairs={{0,24},{8,16},{16,8},{24,0},{1,25},{9,17},{17,9},{25,1},{2,26},{10... | collective-permute-start | bytes 589832 | tf_op jit(solution)/shard_map/ppermute | solution.py:302
  15.4 23.1 %collective-permute-start.4 = (bf16[32,1024]{1,0:T(8,128)(2,1)S(1)}, bf16[32,1024]{1,0:T(8,128)(2,1)S(1)}, u32[]{:S(2)}, u32[]{:S(2)}) collective-permute-start(bf16[32,1024]{1,0:T(8,128)(2,1)S(1)} %get-tuple-element.16), channel_id=1, source_target_pairs={{0,24},{1,25},{2,26},{3,27},{4,28},{5,29},{6,30},{7,31},{8,16},{9,... | collective-permute-start | bytes 196616 | tf_op jit(solution)/shard_map/ppermute | solution.py:273
  16.8 22.3 %collective-permute-start.5 = (bf16[32,1024]{1,0:T(8,128)(2,1)S(1)}, bf16[32,1024]{1,0:T(8,128)(2,1)S(1)}, u32[]{:S(2)}, u32[]{:S(2)}) collective-permute-start(bf16[32,1024]{1,0:T(8,128)(2,1)S(1)} %get-tuple-element.17), channel_id=1, source_target_pairs={{0,25},{1,24},{2,27},{3,26},{4,29},{5,28},{6,31},{7,30},{8,17},{9,... | collective-permute-start | bytes 196616 | tf_op jit(solution)/shard_map/ppermute | solution.py:273
  32.3 8.3 %collective-permute-start.6 = (bf16[32,1024]{1,0:T(8,128)(2,1)S(1)}, bf16[32,1024]{1,0:T(8,128)(2,1)S(1)}, u32[]{:S(2)}, u32[]{:S(2)}) collective-permute-start(bf16[32,1024]{1,0:T(8,128)(2,1)S(1)} %get-tuple-element.18), channel_id=1, source_target_pairs={{0,26},{1,27},{2,24},{3,25},{4,30},{5,31},{6,28},{7,29},{8,18},{9,... | collective-permute-start | bytes 196616 | tf_op jit(solution)/shard_map/ppermute | solution.py:273
  32.3 8.2 %collective-permute-start.7 = (bf16[32,1024]{1,0:T(8,128)(2,1)S(1)}, bf16[32,1024]{1,0:T(8,128)(2,1)S(1)}, u32[]{:S(2)}, u32[]{:S(2)}) collective-permute-start(bf16[32,1024]{1,0:T(8,128)(2,1)S(1)} %get-tuple-element.19), channel_id=1, source_target_pairs={{0,27},{1,26},{2,25},{3,24},{4,31},{5,30},{6,29},{7,28},{8,19},{9,... | collective-permute-start | bytes 196616 | tf_op jit(solution)/shard_map/ppermute | solution.py:273
  38.5 4.7 %collective-permute-start.2 = (bf16[32,1024]{1,0:T(8,128)(2,1)S(1)}, bf16[32,1024]{1,0:T(8,128)(2,1)S(1)}, u32[]{:S(2)}, u32[]{:S(2)}) collective-permute-start(bf16[32,1024]{1,0:T(8,128)(2,1)S(1)} %slice.8), channel_id=1, source_target_pairs={{0,1},{1,0},{2,3},{3,2},{4,5},{5,4},{6,7},{7,6},{8,9},{9,8},{10,11... | collective-permute-start | bytes 196616 | tf_op jit(solution)/shard_map/ppermute | solution.py:273
  39.1 5.5 %collective-permute-start.3 = (bf16[32,1024]{1,0:T(8,128)(2,1)S(1)}, bf16[32,1024]{1,0:T(8,128)(2,1)S(1)}, u32[]{:S(2)}, u32[]{:S(2)}) collective-permute-start(bf16[32,1024]{1,0:T(8,128)(2,1)S(1)} %slice.9), channel_id=1, source_target_pairs={{0,1},{1,0},{2,3},{3,2},{4,5},{5,4},{6,7},{7,6},{8,9},{9,8},{10,11... | collective-permute-start | bytes 196616 | tf_op jit(solution)/shard_map/ppermute | solution.py:273
where the time goes:
time: 48.7 us; the launch traced here: 48.5 us
  starting transfers between devices  23.5 us (48%)
  waiting for transfers between devices  18.3 us (38%)
  Pallas kernels  6.06 us (12%)
  between operations  0.67 us (1%)
    ppermute x8, waiting for transfers between devices, direct(): return lax.ppermute(block, ('section', 'expert'), pairs)  18.3 us
    ppermute x8, starting transfers between devices, direct(): return lax.ppermute(block, ('section', 'expert'), pairs)  15.3 us
    all_to_all x1, starting transfers between devices, exchange(): lax.all_to_all(blocks, ('section', 'expert'), split_axis=0, concat_axis=0...  7.82 us
    pallas_call x2, Pallas kernels, whole_call(): pl.pallas_call(body, out_shape=out_shape, in_specs=[in_spec] * len(operan...  6.06 us
  transfers between devices with their start and end apart: 10, of which 3 were waited for; matrix products, arithmetic and copies ran while one was open for 0% of the time, Pallas kernels for 0%

commit v1 on v0

--- a/solution.py
+++ b/solution.py
@@ -208,7 +208,7 @@
                 for block in (pair[:capacity, cols], relay[:, cols])
             ]
             + [joint_ref[1 - half, :, cols]]
-            + [ref[:, cols] for ref in single_refs],
+            + [ref[:capacity, cols] for ref in single_refs],
             axis=0,
         )
         accum = jnp.dot(hidden, rows, preferred_element_type=jnp.float32)
@@ -279,6 +279,10 @@
     )
 
 
+def near_bundles(near_peers):
+    return [(distance, 2) for distance in range(0, near_peers, 2)]
+
+
 def splits(peers, capacity):
     return peers > 2 and peers & (peers - 1) == 0 and capacity % TILE_ROWS == 0
 
@@ -316,7 +320,7 @@
         joint, *singles, near_hidden, turned = whole_call(
             functools.partial(pack_split_kernel, peers, capacity, sections),
             (shaped(2, near_peers * capacity, width),) + (landing(2 * capacity, width),) * (near_peers // 2)
-            + (landing(capacity, width),) * near_peers
+            + tuple(landing(size * capacity, width) for _, size in near_bundles(near_peers))
             + (landing(height, slots),) * 2,
             (ids, grad_rows[0], saved_hidden.reshape(2, slots, height)),
             (
@@ -327,14 +331,17 @@
                 pltpu.SemaphoreType.DMA((5, 2)),
             ),
             in_spec=ANY,
-            out_spec=(ANY,) + (VMEM,) * (near_peers // 2 + near_peers + 2),
+            out_spec=(ANY,) + (VMEM,) * (near_peers // 2 + len(near_bundles(near_peers)) + 2),
         )
         pairs = near_peers // 2
         landed, relayed, mirrored = [], [], []
         for index, block in enumerate(singles[:pairs]):
             landed.append(direct(block, sections, peers, near_peers + 2 * index, False))
-        for index, block in enumerate(singles[pairs:]):
-            mirrored.append(direct(block, sections, peers, index, True))
+        for (distance, size), block in zip(near_bundles(near_peers), singles[pairs:]):
+            block = direct(block, sections, peers, distance, True)
+            mirrored.append(block)
+            if size == 2:
+                mirrored.append(direct(block[capacity:], sections, peers, 1, False))
         for block in landed:
             relayed.append(direct(block[capacity:], sections, peers, 1, False))
         far_hidden = hidden_over(turned)

time: 48.7 us -> 45.9 us (0.943)
  the two profiles are of different devices: /device:TPU:0 before, /device:TPU:2 now
where the time goes in v1:
time: 45.9 us; the launch traced here: 45.6 us
  waiting for transfers between devices  22.5 us (49%)
  starting transfers between devices  16.4 us (36%)
  Pallas kernels  6.05 us (13%)
  between operations  0.67 us (1%)
    ppermute x8, waiting for transfers between devices, direct(): return lax.ppermute(block, ('section', 'expert'), pairs)  22.5 us
    ppermute x8, starting transfers between devices, direct(): return lax.ppermute(block, ('section', 'expert'), pairs)  10.4 us
    pallas_call x2, Pallas kernels, whole_call(): pl.pallas_call(body, out_shape=out_shape, in_specs=[in_spec] * len(operan...  6.05 us
    all_to_all x1, starting transfers between devices, exchange(): lax.all_to_all(blocks, ('section', 'expert'), split_axis=0, concat_axis=0...  6.03 us
  transfers between devices with their start and end apart: 10, of which 5 were waited for; matrix products, arithmetic and copies ran while one was open for 0% of the time, Pallas kernels for 0%

profile of v1, /device:TPU:2, one launch (start us, length us, event | category | flops | bytes accessed | tf_op | source)
XLA Modules:
  0.0 45.6 jit_solution(8013470063654980772)
XLA Ops:
  0.6 2.2 %shard_map.59 = (bf16[2,128,1024]{2,1,0:T(8,128)(2,1)}, bf16[64,1024]{1,0:T(8,128)(2,1)S(1)}, bf16[64,1024]{1,0:T(8,128)(2,1)S(1)}, bf16[64,1024]{1,0:T(8,128)(2...) custom-call(s32[2,1,128]{2,1,0:T(1,128)} %bitcast.13, ...), custom_call_target="tpu_custom_call" | custom-call | tf_op jit(solution)/shard_map/pallas_call | solution.py:26
  2.8 0.0 copy-start
  2.8 6.0 %all-to-all-start = ((bf16[8,32,1024]{2,1,0:T(8,128)(2,1)}), bf16[8,32,1024]{2,1,0:T(8,128)(2,1)S(1)}, u32[]{:S(2)}, u32[]{:S(2)}) async-start(bf16[8,32,1024]{2,1,0:T(8,128)(2,1)} %bitcast.11), calls=%async_computation | async-start | bytes 1048576 | tf_op jit(solution)/shard_map/all_to_all | solution.py:277
  8.9 3.5 %collective-permute-start = (bf16[64,1024]{1,0:T(8,128)(2,1)S(1)}, bf16[64,1024]{1,0:T(8,128)(2,1)S(1)}, u32[]{:S(2)}, u32[]{:S(2)}) collective-permute-start(bf16[64,1024]{1,0:T(8,128)(2,1)S(1)} %get-tuple-element.12), channel_id=1, source_target_pairs={{0,4},{1,5},{2,6},{3,7},{4,0},{5,1},{6,2},{7,3},{8,12},{9,13},{10,... | collective-permute-start | bytes 393224 | tf_op jit(solution)/shard_map/ppermute | solution.py:273
  12.4 0.9 %collective-permute-start.1 = (bf16[64,1024]{1,0:T(8,128)(2,1)S(1)}, bf16[64,1024]{1,0:T(8,128)(2,1)S(1)}, u32[]{:S(2)}, u32[]{:S(2)}) collective-permute-start(bf16[64,1024]{1,0:T(8,128)(2,1)S(1)} %get-tuple-element.13), channel_id=1, source_target_pairs={{0,6},{1,7},{2,4},{3,5},{4,2},{5,3},{6,0},{7,1},{8,14},{9,15},{10,... | collective-permute-start | bytes 393224 | tf_op jit(solution)/shard_map/ppermute | solution.py:273
  13.3 0.3 collective-permute-start.4
  13.5 1.5 %collective-permute-start.6 = (bf16[64,1024]{1,0:T(8,128)(2,1)S(1)}, bf16[64,1024]{1,0:T(8,128)(2,1)S(1)}, u32[]{:S(2)}, u32[]{:S(2)}) collective-permute-start(bf16[64,1024]{1,0:T(8,128)(2,1)S(1)} %get-tuple-element.15), channel_id=1, source_target_pairs={{0,26},{1,27},{2,24},{3,25},{4,30},{5,31},{6,28},{7,29},{8,18},{9,... | collective-permute-start | bytes 393224 | tf_op jit(solution)/shard_map/ppermute | solution.py:273
  15.0 0.0 collective-permute-start.8
  15.0 18.7 %collective-permute-done.refs_0_ = bf16[64,1024]{1,0:T(8,128)(2,1)S(1)} collective-permute-done((bf16[64,1024]{1,0:T(8,128)(2,1)S(1)}, bf16[64,1024]{1,0:T(8,128)(2,1)S(1)}, u32[]{:S(2)}, u32[]{:S(2)}) %collective-permute-start) | collective-permute-done | bytes 131104 | tf_op jit(solution)/shard_map/ppermute | solution.py:273
  33.8 1.5 %collective-permute-start.2 = (bf16[32,1024]{1,0:T(8,128)(2,1)S(1)}, bf16[32,1024]{1,0:T(8,128)(2,1)S(1)}, u32[]{:S(2)}, u32[]{:S(2)}) collective-permute-start(bf16[32,1024]{1,0:T(8,128)(2,1)S(1)} %slice.16), channel_id=1, source_target_pairs={{0,1},{1,0},{2,3},{3,2},{4,5},{5,4},{6,7},{7,6},{8,9},{9,8},{10,11... | collective-permute-start | bytes 196616 | tf_op jit(solution)/shard_map/ppermute | solution.py:273
  35.2 0.0 collective-permute-done.1.refs_1_
  35.2 0.6 %collective-permute-start.3 = (bf16[32,1024]{1,0:T(8,128)(2,1)S(1)}, bf16[32,1024]{1,0:T(8,128)(2,1)S(1)}, u32[]{:S(2)}, u32[]{:S(2)}) collective-permute-start(bf16[32,1024]{1,0:T(8,128)(2,1)S(1)} %slice.17), channel_id=1, source_target_pairs={{0,1},{1,0},{2,3},{3,2},{4,5},{5,4},{6,7},{7,6},{8,9},{9,8},{10,11... | collective-permute-start | bytes 196616 | tf_op jit(solution)/shard_map/ppermute | solution.py:273
  35.9 0.0 collective-permute-done.4.refs_4_
  35.9 1.5 %collective-permute-start.5 = (bf16[32,1024]{1,0:T(8,128)(2,1)S(1)}, bf16[32,1024]{1,0:T(8,128)(2,1)S(1)}, u32[]{:S(2)}, u32[]{:S(2)}) collective-permute-start(bf16[32,1024]{1,0:T(8,128)(2,1)S(1)} %slice.18), channel_id=1, source_target_pairs={{0,1},{1,0},{2,3},{3,2},{4,5},{5,4},{6,7},{7,6},{8,9},{9,8},{10,11... | collective-permute-start | bytes 196616 | tf_op jit(solution)/shard_map/ppermute | solution.py:273
  37.4 0.0 collective-permute-done.6.refs_6_
  37.4 0.6 %collective-permute-start.7 = (bf16[32,1024]{1,0:T(8,128)(2,1)S(1)}, bf16[32,1024]{1,0:T(8,128)(2,1)S(1)}, u32[]{:S(2)}, u32[]{:S(2)}) collective-permute-start(bf16[32,1024]{1,0:T(8,128)(2,1)S(1)} %slice.19), channel_id=1, source_target_pairs={{0,1},{1,0},{2,3},{3,2},{4,5},{5,4},{6,7},{7,6},{8,9},{9,8},{10,11... | collective-permute-start | bytes 196616 | tf_op jit(solution)/shard_map/ppermute | solution.py:273
  38.1 0.6 %collective-permute-done.2.refs_2_ = bf16[32,1024]{1,0:T(8,128)(2,1)S(1)} collective-permute-done((bf16[32,1024]{1,0:T(8,128)(2,1)S(1)}, bf16[32,1024]{1,0:T(8,128)(2,1)S(1)}, u32[]{:S(2)}, u32[]{:S(2)}) %collective-permute-start.2) | collective-permute-done | bytes 65568 | tf_op jit(solution)/shard_map/ppermute | solution.py:273
  38.6 1.0 %collective-permute-done.3.refs_3_ = bf16[32,1024]{1,0:T(8,128)(2,1)S(1)} collective-permute-done((bf16[32,1024]{1,0:T(8,128)(2,1)S(1)}, bf16[32,1024]{1,0:T(8,128)(2,1)S(1)}, u32[]{:S(2)}, u32[]{:S(2)}) %collective-permute-start.3) | collective-permute-done | bytes 65568 | tf_op jit(solution)/shard_map/ppermute | solution.py:273
  39.6 0.7 %collective-permute-done.5.refs_5_ = bf16[32,1024]{1,0:T(8,128)(2,1)S(1)} collective-permute-done((bf16[32,1024]{1,0:T(8,128)(2,1)S(1)}, bf16[32,1024]{1,0:T(8,128)(2,1)S(1)}, u32[]{:S(2)}, u32[]{:S(2)}) %collective-permute-start.5) | collective-permute-done | bytes 65568 | tf_op jit(solution)/shard_map/ppermute | solution.py:273
  40.3 1.5 %collective-permute-done.7.refs_7_ = bf16[32,1024]{1,0:T(8,128)(2,1)S(1)} collective-permute-done((bf16[32,1024]{1,0:T(8,128)(2,1)S(1)}, bf16[32,1024]{1,0:T(8,128)(2,1)S(1)}, u32[]{:S(2)}, u32[]{:S(2)}) %collective-permute-start.7) | collective-permute-done | bytes 65568 | tf_op jit(solution)/shard_map/ppermute | solution.py:273
  41.8 0.0 collective-permute-done.8.refs_9_
  41.8 0.0 all-to-all-done
  41.8 0.0 copy-done
  41.8 3.9 %shard_map.60 = (bf16[384,1024]{1,0:T(8,128)(2,1)}, bf16[384,1024]{1,0:T(8,128)(2,1)}) custom-call(bf16[2,128,1024]{2,1,0:T(8,128)(2,1)S(1)} %bitcast.8, bf16[64,1024]{1,0:T(8,128)(2,1)S(1)} %collective-permute-done.refs_0_, bf16[64,1024]{1,0:T(8,128)(2,1)S(1)} %collective-permute-done.1.refs_1_, bf16[32,1024]{1,0:T(8,128)(2,1)S(1)} %collective-permute-done.2.refs_2_, ...), custom_call_target="tpu_custom_call" | custom-call | tf_op jit(solution)/shard_map/pallas_call | solution.py:26
  (4 shorter events, 0.0 us)
Async XLA Ops:
  2.8 38.9 %copy-start = (bf16[1,1,384,1024]{3,2,1,0:T(8,128)(2,1)S(1)}, bf16[1,1,384,1024]{3,2,1,0:T(8,128)(2,1)}, u32[]{:S(2)}) copy-start(bf16[1,1,384,1024]{3,2,1,0:T(8,128)(2,1)} %param.7) | copy-start | bytes 2359300
  2.8 38.9 %all-to-all-start = ((bf16[8,32,1024]{2,1,0:T(8,128)(2,1)}), bf16[8,32,1024]{2,1,0:T(8,128)(2,1)S(1)}, u32[]{:S(2)}, u32[]{:S(2)}) async-start(bf16[8,32,1024]{2,1,0:T(8,128)(2,1)} %bitcast.11), calls=%async_computation | async-start | bytes 1048576 | tf_op jit(solution)/shard_map/all_to_all | solution.py:277
  8.9 24.9 %collective-permute-start = (bf16[64,1024]{1,0:T(8,128)(2,1)S(1)}, bf16[64,1024]{1,0:T(8,128)(2,1)S(1)}, u32[]{:S(2)}, u32[]{:S(2)}) collective-permute-start(bf16[64,1024]{1,0:T(8,128)(2,1)S(1)} %get-tuple-element.12), channel_id=1, source_target_pairs={{0,4},{1,5},{2,6},{3,7},{4,0},{5,1},{6,2},{7,3},{8,12},{9,13},{10,... | collective-permute-start | bytes 393224 | tf_op jit(solution)/shard_map/ppermute | solution.py:273
  12.4 22.9 %collective-permute-start.1 = (bf16[64,1024]{1,0:T(8,128)(2,1)S(1)}, bf16[64,1024]{1,0:T(8,128)(2,1)S(1)}, u32[]{:S(2)}, u32[]{:S(2)}) collective-permute-start(bf16[64,1024]{1,0:T(8,128)(2,1)S(1)} %get-tuple-element.13), channel_id=1, source_target_pairs={{0,6},{1,7},{2,4},{3,5},{4,2},{5,3},{6,0},{7,1},{8,14},{9,15},{10,... | collective-permute-start | bytes 393224 | tf_op jit(solution)/shard_map/ppermute | solution.py:273
  13.3 22.6 %collective-permute-start.4 = (bf16[64,1024]{1,0:T(8,128)(2,1)S(1)}, bf16[64,1024]{1,0:T(8,128)(2,1)S(1)}, u32[]{:S(2)}, u32[]{:S(2)}) collective-permute-start(bf16[64,1024]{1,0:T(8,128)(2,1)S(1)} %get-tuple-element.14), channel_id=1, source_target_pairs={{0,24},{1,25},{2,26},{3,27},{4,28},{5,29},{6,30},{7,31},{8,16},{9,... | collective-permute-start | bytes 393224 | tf_op jit(solution)/shard_map/ppermute | solution.py:273
  13.5 23.9 %collective-permute-start.6 = (bf16[64,1024]{1,0:T(8,128)(2,1)S(1)}, bf16[64,1024]{1,0:T(8,128)(2,1)S(1)}, u32[]{:S(2)}, u32[]{:S(2)}) collective-permute-start(bf16[64,1024]{1,0:T(8,128)(2,1)S(1)} %get-tuple-element.15), channel_id=1, source_target_pairs={{0,26},{1,27},{2,24},{3,25},{4,30},{5,31},{6,28},{7,29},{8,18},{9,... | collective-permute-start | bytes 393224 | tf_op jit(solution)/shard_map/ppermute | solution.py:273
  15.0 26.7 %collective-permute-start.8 = (bf16[384,256]{1,0:T(8,128)(2,1)S(1)}, bf16[384,256]{1,0:T(8,128)(2,1)S(1)}, u32[]{:S(2)}, u32[]{:S(2)}) collective-permute-start(bf16[384,256]{1,0:T(8,128)(2,1)S(1)} %get-tuple-element.17), channel_id=1, source_target_pairs={{0,24},{8,16},{16,8},{24,0},{1,25},{9,17},{17,9},{25,1},{2,26},{10... | collective-permute-start | bytes 589832 | tf_op jit(solution)/shard_map/ppermute | solution.py:306
  33.8 4.9 %collective-permute-start.2 = (bf16[32,1024]{1,0:T(8,128)(2,1)S(1)}, bf16[32,1024]{1,0:T(8,128)(2,1)S(1)}, u32[]{:S(2)}, u32[]{:S(2)}) collective-permute-start(bf16[32,1024]{1,0:T(8,128)(2,1)S(1)} %slice.16), channel_id=1, source_target_pairs={{0,1},{1,0},{2,3},{3,2},{4,5},{5,4},{6,7},{7,6},{8,9},{9,8},{10,11... | collective-permute-start | bytes 196616 | tf_op jit(solution)/shard_map/ppermute | solution.py:273
  35.2 4.3 %collective-permute-start.3 = (bf16[32,1024]{1,0:T(8,128)(2,1)S(1)}, bf16[32,1024]{1,0:T(8,128)(2,1)S(1)}, u32[]{:S(2)}, u32[]{:S(2)}) collective-permute-start(bf16[32,1024]{1,0:T(8,128)(2,1)S(1)} %slice.17), channel_id=1, source_target_pairs={{0,1},{1,0},{2,3},{3,2},{4,5},{5,4},{6,7},{7,6},{8,9},{9,8},{10,11... | collective-permute-start | bytes 196616 | tf_op jit(solution)/shard_map/ppermute | solution.py:273
  35.9 4.4 %collective-permute-start.5 = (bf16[32,1024]{1,0:T(8,128)(2,1)S(1)}, bf16[32,1024]{1,0:T(8,128)(2,1)S(1)}, u32[]{:S(2)}, u32[]{:S(2)}) collective-permute-start(bf16[32,1024]{1,0:T(8,128)(2,1)S(1)} %slice.18), channel_id=1, source_target_pairs={{0,1},{1,0},{2,3},{3,2},{4,5},{5,4},{6,7},{7,6},{8,9},{9,8},{10,11... | collective-permute-start | bytes 196616 | tf_op jit(solution)/shard_map/ppermute | solution.py:273
  37.4 4.3 %collective-permute-start.7 = (bf16[32,1024]{1,0:T(8,128)(2,1)S(1)}, bf16[32,1024]{1,0:T(8,128)(2,1)S(1)}, u32[]{:S(2)}, u32[]{:S(2)}) collective-permute-start(bf16[32,1024]{1,0:T(8,128)(2,1)S(1)} %slice.19), channel_id=1, source_target_pairs={{0,1},{1,0},{2,3},{3,2},{4,5},{5,4},{6,7},{7,6},{8,9},{9,8},{10,11... | collective-permute-start | bytes 196616 | tf_op jit(solution)/shard_map/ppermute | solution.py:273

commit v2 on v1

--- a/solution.py
+++ b/solution.py
@@ -11,6 +11,7 @@
 ITERS = 2
 TILE_ROWS = 16
 PIECES = 1
+WIDE, NARROW = 512, 256
 
 momentum_decay = 0.95
 coef_first = 3.4445
@@ -188,16 +189,17 @@
     capacity = relay_refs[0].shape[0]
     half = own_half(sections)
     height, width = momentum_ref.shape
-    chunk = min(256, width)
-    columns = [pl.ds(start, chunk) for start in range(0, width, chunk)]
-
-    def copies(ref, hbm, row):
+    chunk = min(WIDE, width)
+    spans = lambda size: [pl.ds(start, size) for start in range(0, width, size)]
+    columns, narrow = spans(chunk), spans(min(NARROW, width))
+
+    def copies(ref, hbm, row, columns):
         return [
             pltpu.make_async_copy(ref.at[:, cols], hbm.at[:, cols], sems.at[row, index])
             for index, cols in enumerate(columns)
         ]
 
-    new_copies, step_copies = copies(new_ref, new_hbm, 0), copies(step_ref, step_hbm, 1)
+    new_copies, step_copies = copies(new_ref, new_hbm, 0, columns), copies(step_ref, step_hbm, 1, narrow)
     hidden = jnp.concatenate([near_ref[...], far_ref[...]], axis=1)
     for cols, copy in zip(columns, new_copies):
         rows = jnp.concatenate(
@@ -235,12 +237,13 @@
         factor = (
             (coef_second / coef_first) * gram.astype(jnp.float32) + (coef_third / coef_first) * square
         ).astype(jnp.bfloat16)
-        for cols, copy in zip(columns, step_copies):
+        final = iteration == ITERS - 1
+        for index, cols in enumerate(narrow if final else columns):
             block = source_ref[:, cols]
             applied = jnp.dot(factor, block, preferred_element_type=jnp.float32)
             step_ref[:, cols] = (scale * (block.astype(jnp.float32) + applied)).astype(jnp.bfloat16)
-            if iteration == ITERS - 1:
-                copy.start()
+            if final:
+                step_copies[index].start()
     for copy in new_copies + step_copies:
         copy.wait()
 
@@ -351,7 +354,7 @@
         scratch = (
             pltpu.VMEM(momentum.shape[2:], jnp.bfloat16),
             pltpu.VMEM(momentum.shape[2:], jnp.bfloat16),
-            pltpu.SemaphoreType.DMA((2, pl.cdiv(width, 256))),
+            pltpu.SemaphoreType.DMA((2, pl.cdiv(width, min(WIDE, NARROW)))),
         )
     new_momentum, update_step = whole_call(
         body, outs, tuple(map(in_vmem, operands)), scratch,

time: 45.9 us -> 45.8 us (level)
  no operation moved by 1% of the time
where the time goes in v2:
time: 45.8 us; the launch traced here: 45.6 us
  waiting for transfers between devices  22.5 us (49%)
  starting transfers between devices  16.4 us (36%)
  Pallas kernels  5.99 us (13%)
  between operations  0.67 us (1%)
    ppermute x8, waiting for transfers between devices, direct(): return lax.ppermute(block, ('section', 'expert'), pairs)  22.5 us
    ppermute x8, starting transfers between devices, direct(): return lax.ppermute(block, ('section', 'expert'), pairs)  10.4 us
    all_to_all x1, starting transfers between devices, exchange(): lax.all_to_all(blocks, ('section', 'expert'), split_axis=0, concat_axis=0...  6.03 us
    pallas_call x2, Pallas kernels, whole_call(): pl.pallas_call(body, out_shape=out_shape, in_specs=[in_spec] * len(operan...  5.99 us
  transfers between devices with their start and end apart: 10, of which 5 were waited for; matrix products, arithmetic and copies ran while one was open for 0% of the time, Pallas kernels for 0%

profile of v2, /device:TPU:2, one launch (start us, length us, event | category | flops | bytes accessed | tf_op | source)
XLA Modules:
  0.0 45.6 jit_solution(8874802316000040452)
XLA Ops:
  0.6 2.2 %shard_map.59 = (bf16[2,128,1024]{2,1,0:T(8,128)(2,1)}, bf16[64,1024]{1,0:T(8,128)(2,1)S(1)}, bf16[64,1024]{1,0:T(8,128)(2,1)S(1)}, bf16[64,1024]{1,0:T(8,128)(2...) custom-call(s32[2,1,128]{2,1,0:T(1,128)} %bitcast.13, ...), custom_call_target="tpu_custom_call" | custom-call | tf_op jit(solution)/shard_map/pallas_call | solution.py:27
  2.8 0.0 copy-start
  2.8 6.0 %all-to-all-start = ((bf16[8,32,1024]{2,1,0:T(8,128)(2,1)}), bf16[8,32,1024]{2,1,0:T(8,128)(2,1)S(1)}, u32[]{:S(2)}, u32[]{:S(2)}) async-start(bf16[8,32,1024]{2,1,0:T(8,128)(2,1)} %bitcast.11), calls=%async_computation | async-start | bytes 1048576 | tf_op jit(solution)/shard_map/all_to_all | solution.py:280
  8.9 3.5 %collective-permute-start = (bf16[64,1024]{1,0:T(8,128)(2,1)S(1)}, bf16[64,1024]{1,0:T(8,128)(2,1)S(1)}, u32[]{:S(2)}, u32[]{:S(2)}) collective-permute-start(bf16[64,1024]{1,0:T(8,128)(2,1)S(1)} %get-tuple-element.12), channel_id=1, source_target_pairs={{0,4},{1,5},{2,6},{3,7},{4,0},{5,1},{6,2},{7,3},{8,12},{9,13},{10,... | collective-permute-start | bytes 393224 | tf_op jit(solution)/shard_map/ppermute | solution.py:276
  12.4 0.9 %collective-permute-start.1 = (bf16[64,1024]{1,0:T(8,128)(2,1)S(1)}, bf16[64,1024]{1,0:T(8,128)(2,1)S(1)}, u32[]{:S(2)}, u32[]{:S(2)}) collective-permute-start(bf16[64,1024]{1,0:T(8,128)(2,1)S(1)} %get-tuple-element.13), channel_id=1, source_target_pairs={{0,6},{1,7},{2,4},{3,5},{4,2},{5,3},{6,0},{7,1},{8,14},{9,15},{10,... | collective-permute-start | bytes 393224 | tf_op jit(solution)/shard_map/ppermute | solution.py:276
  13.3 0.3 collective-permute-start.4
  13.5 1.5 %collective-permute-start.6 = (bf16[64,1024]{1,0:T(8,128)(2,1)S(1)}, bf16[64,1024]{1,0:T(8,128)(2,1)S(1)}, u32[]{:S(2)}, u32[]{:S(2)}) collective-permute-start(bf16[64,1024]{1,0:T(8,128)(2,1)S(1)} %get-tuple-element.15), channel_id=1, source_target_pairs={{0,26},{1,27},{2,24},{3,25},{4,30},{5,31},{6,28},{7,29},{8,18},{9,... | collective-permute-start | bytes 393224 | tf_op jit(solution)/shard_map/ppermute | solution.py:276
  15.0 0.0 collective-permute-start.8
  15.0 18.7 %collective-permute-done.refs_0_ = bf16[64,1024]{1,0:T(8,128)(2,1)S(1)} collective-permute-done((bf16[64,1024]{1,0:T(8,128)(2,1)S(1)}, bf16[64,1024]{1,0:T(8,128)(2,1)S(1)}, u32[]{:S(2)}, u32[]{:S(2)}) %collective-permute-start) | collective-permute-done | bytes 131104 | tf_op jit(solution)/shard_map/ppermute | solution.py:276
  33.8 1.5 %collective-permute-start.2 = (bf16[32,1024]{1,0:T(8,128)(2,1)S(1)}, bf16[32,1024]{1,0:T(8,128)(2,1)S(1)}, u32[]{:S(2)}, u32[]{:S(2)}) collective-permute-start(bf16[32,1024]{1,0:T(8,128)(2,1)S(1)} %slice.16), channel_id=1, source_target_pairs={{0,1},{1,0},{2,3},{3,2},{4,5},{5,4},{6,7},{7,6},{8,9},{9,8},{10,11... | collective-permute-start | bytes 196616 | tf_op jit(solution)/shard_map/ppermute | solution.py:276
  35.2 0.0 collective-permute-done.1.refs_1_
  35.2 0.6 %collective-permute-start.3 = (bf16[32,1024]{1,0:T(8,128)(2,1)S(1)}, bf16[32,1024]{1,0:T(8,128)(2,1)S(1)}, u32[]{:S(2)}, u32[]{:S(2)}) collective-permute-start(bf16[32,1024]{1,0:T(8,128)(2,1)S(1)} %slice.17), channel_id=1, source_target_pairs={{0,1},{1,0},{2,3},{3,2},{4,5},{5,4},{6,7},{7,6},{8,9},{9,8},{10,11... | collective-permute-start | bytes 196616 | tf_op jit(solution)/shard_map/ppermute | solution.py:276
  35.9 0.0 collective-permute-done.4.refs_4_
  35.9 1.5 %collective-permute-start.5 = (bf16[32,1024]{1,0:T(8,128)(2,1)S(1)}, bf16[32,1024]{1,0:T(8,128)(2,1)S(1)}, u32[]{:S(2)}, u32[]{:S(2)}) collective-permute-start(bf16[32,1024]{1,0:T(8,128)(2,1)S(1)} %slice.18), channel_id=1, source_target_pairs={{0,1},{1,0},{2,3},{3,2},{4,5},{5,4},{6,7},{7,6},{8,9},{9,8},{10,11... | collective-permute-start | bytes 196616 | tf_op jit(solution)/shard_map/ppermute | solution.py:276
  37.4 0.0 collective-permute-done.6.refs_6_
  37.4 0.6 %collective-permute-start.7 = (bf16[32,1024]{1,0:T(8,128)(2,1)S(1)}, bf16[32,1024]{1,0:T(8,128)(2,1)S(1)}, u32[]{:S(2)}, u32[]{:S(2)}) collective-permute-start(bf16[32,1024]{1,0:T(8,128)(2,1)S(1)} %slice.19), channel_id=1, source_target_pairs={{0,1},{1,0},{2,3},{3,2},{4,5},{5,4},{6,7},{7,6},{8,9},{9,8},{10,11... | collective-permute-start | bytes 196616 | tf_op jit(solution)/shard_map/ppermute | solution.py:276
  38.1 0.6 %collective-permute-done.2.refs_2_ = bf16[32,1024]{1,0:T(8,128)(2,1)S(1)} collective-permute-done((bf16[32,1024]{1,0:T(8,128)(2,1)S(1)}, bf16[32,1024]{1,0:T(8,128)(2,1)S(1)}, u32[]{:S(2)}, u32[]{:S(2)}) %collective-permute-start.2) | collective-permute-done | bytes 65568 | tf_op jit(solution)/shard_map/ppermute | solution.py:276
  38.6 1.0 %collective-permute-done.3.refs_3_ = bf16[32,1024]{1,0:T(8,128)(2,1)S(1)} collective-permute-done((bf16[32,1024]{1,0:T(8,128)(2,1)S(1)}, bf16[32,1024]{1,0:T(8,128)(2,1)S(1)}, u32[]{:S(2)}, u32[]{:S(2)}) %collective-permute-start.3) | collective-permute-done | bytes 65568 | tf_op jit(solution)/shard_map/ppermute | solution.py:276
  39.6 0.7 %collective-permute-done.5.refs_5_ = bf16[32,1024]{1,0:T(8,128)(2,1)S(1)} collective-permute-done((bf16[32,1024]{1,0:T(8,128)(2,1)S(1)}, bf16[32,1024]{1,0:T(8,128)(2,1)S(1)}, u32[]{:S(2)}, u32[]{:S(2)}) %collective-permute-start.5) | collective-permute-done | bytes 65568 | tf_op jit(solution)/shard_map/ppermute | solution.py:276
  40.3 1.5 %collective-permute-done.7.refs_7_ = bf16[32,1024]{1,0:T(8,128)(2,1)S(1)} collective-permute-done((bf16[32,1024]{1,0:T(8,128)(2,1)S(1)}, bf16[32,1024]{1,0:T(8,128)(2,1)S(1)}, u32[]{:S(2)}, u32[]{:S(2)}) %collective-permute-start.7) | collective-permute-done | bytes 65568 | tf_op jit(solution)/shard_map/ppermute | solution.py:276
  41.8 0.0 collective-permute-done.8.refs_9_
  41.8 0.0 all-to-all-done
  41.8 0.0 copy-done
  41.8 3.8 %shard_map.60 = (bf16[384,1024]{1,0:T(8,128)(2,1)}, bf16[384,1024]{1,0:T(8,128)(2,1)}) custom-call(bf16[2,128,1024]{2,1,0:T(8,128)(2,1)S(1)} %bitcast.8, bf16[64,1024]{1,0:T(8,128)(2,1)S(1)} %collective-permute-done.refs_0_, bf16[64,1024]{1,0:T(8,128)(2,1)S(1)} %collective-permute-done.1.refs_1_, bf16[32,1024]{1,0:T(8,128)(2,1)S(1)} %collective-permute-done.2.refs_2_, ...), custom_call_target="tpu_custom_call" | custom-call | tf_op jit(solution)/shard_map/pallas_call | solution.py:27
  (4 shorter events, 0.0 us)
Async XLA Ops:
  2.8 38.9 %copy-start = (bf16[1,1,384,1024]{3,2,1,0:T(8,128)(2,1)S(1)}, bf16[1,1,384,1024]{3,2,1,0:T(8,128)(2,1)}, u32[]{:S(2)}) copy-start(bf16[1,1,384,1024]{3,2,1,0:T(8,128)(2,1)} %param.7) | copy-start | bytes 2359300
  2.8 38.9 %all-to-all-start = ((bf16[8,32,1024]{2,1,0:T(8,128)(2,1)}), bf16[8,32,1024]{2,1,0:T(8,128)(2,1)S(1)}, u32[]{:S(2)}, u32[]{:S(2)}) async-start(bf16[8,32,1024]{2,1,0:T(8,128)(2,1)} %bitcast.11), calls=%async_computation | async-start | bytes 1048576 | tf_op jit(solution)/shard_map/all_to_all | solution.py:280
  8.9 24.9 %collective-permute-start = (bf16[64,1024]{1,0:T(8,128)(2,1)S(1)}, bf16[64,1024]{1,0:T(8,128)(2,1)S(1)}, u32[]{:S(2)}, u32[]{:S(2)}) collective-permute-start(bf16[64,1024]{1,0:T(8,128)(2,1)S(1)} %get-tuple-element.12), channel_id=1, source_target_pairs={{0,4},{1,5},{2,6},{3,7},{4,0},{5,1},{6,2},{7,3},{8,12},{9,13},{10,... | collective-permute-start | bytes 393224 | tf_op jit(solution)/shard_map/ppermute | solution.py:276
  12.4 22.9 %collective-permute-start.1 = (bf16[64,1024]{1,0:T(8,128)(2,1)S(1)}, bf16[64,1024]{1,0:T(8,128)(2,1)S(1)}, u32[]{:S(2)}, u32[]{:S(2)}) collective-permute-start(bf16[64,1024]{1,0:T(8,128)(2,1)S(1)} %get-tuple-element.13), channel_id=1, source_target_pairs={{0,6},{1,7},{2,4},{3,5},{4,2},{5,3},{6,0},{7,1},{8,14},{9,15},{10,... | collective-permute-start | bytes 393224 | tf_op jit(solution)/shard_map/ppermute | solution.py:276
  13.3 22.6 %collective-permute-start.4 = (bf16[64,1024]{1,0:T(8,128)(2,1)S(1)}, bf16[64,1024]{1,0:T(8,128)(2,1)S(1)}, u32[]{:S(2)}, u32[]{:S(2)}) collective-permute-start(bf16[64,1024]{1,0:T(8,128)(2,1)S(1)} %get-tuple-element.14), channel_id=1, source_target_pairs={{0,24},{1,25},{2,26},{3,27},{4,28},{5,29},{6,30},{7,31},{8,16},{9,... | collective-permute-start | bytes 393224 | tf_op jit(solution)/shard_map/ppermute | solution.py:276
  13.5 23.9 %collective-permute-start.6 = (bf16[64,1024]{1,0:T(8,128)(2,1)S(1)}, bf16[64,1024]{1,0:T(8,128)(2,1)S(1)}, u32[]{:S(2)}, u32[]{:S(2)}) collective-permute-start(bf16[64,1024]{1,0:T(8,128)(2,1)S(1)} %get-tuple-element.15), channel_id=1, source_target_pairs={{0,26},{1,27},{2,24},{3,25},{4,30},{5,31},{6,28},{7,29},{8,18},{9,... | collective-permute-start | bytes 393224 | tf_op jit(solution)/shard_map/ppermute | solution.py:276
  15.0 26.7 %collective-permute-start.8 = (bf16[384,256]{1,0:T(8,128)(2,1)S(1)}, bf16[384,256]{1,0:T(8,128)(2,1)S(1)}, u32[]{:S(2)}, u32[]{:S(2)}) collective-permute-start(bf16[384,256]{1,0:T(8,128)(2,1)S(1)} %get-tuple-element.17), channel_id=1, source_target_pairs={{0,24},{8,16},{16,8},{24,0},{1,25},{9,17},{17,9},{25,1},{2,26},{10... | collective-permute-start | bytes 589832 | tf_op jit(solution)/shard_map/ppermute | solution.py:309
  33.8 4.9 %collective-permute-start.2 = (bf16[32,1024]{1,0:T(8,128)(2,1)S(1)}, bf16[32,1024]{1,0:T(8,128)(2,1)S(1)}, u32[]{:S(2)}, u32[]{:S(2)}) collective-permute-start(bf16[32,1024]{1,0:T(8,128)(2,1)S(1)} %slice.16), channel_id=1, source_target_pairs={{0,1},{1,0},{2,3},{3,2},{4,5},{5,4},{6,7},{7,6},{8,9},{9,8},{10,11... | collective-permute-start | bytes 196616 | tf_op jit(solution)/shard_map/ppermute | solution.py:276
  35.2 4.3 %collective-permute-start.3 = (bf16[32,1024]{1,0:T(8,128)(2,1)S(1)}, bf16[32,1024]{1,0:T(8,128)(2,1)S(1)}, u32[]{:S(2)}, u32[]{:S(2)}) collective-permute-start(bf16[32,1024]{1,0:T(8,128)(2,1)S(1)} %slice.17), channel_id=1, source_target_pairs={{0,1},{1,0},{2,3},{3,2},{4,5},{5,4},{6,7},{7,6},{8,9},{9,8},{10,11... | collective-permute-start | bytes 196616 | tf_op jit(solution)/shard_map/ppermute | solution.py:276
  35.9 4.4 %collective-permute-start.5 = (bf16[32,1024]{1,0:T(8,128)(2,1)S(1)}, bf16[32,1024]{1,0:T(8,128)(2,1)S(1)}, u32[]{:S(2)}, u32[]{:S(2)}) collective-permute-start(bf16[32,1024]{1,0:T(8,128)(2,1)S(1)} %slice.18), channel_id=1, source_target_pairs={{0,1},{1,0},{2,3},{3,2},{4,5},{5,4},{6,7},{7,6},{8,9},{9,8},{10,11... | collective-permute-start | bytes 196616 | tf_op jit(solution)/shard_map/ppermute | solution.py:276
  37.4 4.3 %collective-permute-start.7 = (bf16[32,1024]{1,0:T(8,128)(2,1)S(1)}, bf16[32,1024]{1,0:T(8,128)(2,1)S(1)}, u32[]{:S(2)}, u32[]{:S(2)}) collective-permute-start(bf16[32,1024]{1,0:T(8,128)(2,1)S(1)} %slice.19), channel_id=1, source_target_pairs={{0,1},{1,0},{2,3},{3,2},{4,5},{5,4},{6,7},{7,6},{8,9},{9,8},{10,11... | collective-permute-start | bytes 196616 | tf_op jit(solution)/shard_map/ppermute | solution.py:276
